TPU v7x, 32 devices: a whole 2x2x4 slice. The times are simulated.
32 devices in a mesh: span: 8 (over z, x), slab: 4 (over y, core).
Axes of the slice: x: 2, y: 2, z: 4, core: 2. Of those that a mesh axis runs over, the one named last changes fastest.
Arguments:
- features: float32 [512, 32, 2048], P('slab', None, 'span'), may hold values from -6 to 6
- spectral_weight: float32 [512, 2048], P('span', 'slab'), may hold values from -2.5 to 2.5
- local_weight: float32 [32, 32], replicated, may hold values from -1 to 1
- bias_vector: float32 [32], replicated, may hold values from -1 to 1
Outputs:
- activated: float32 [512, 32, 2048], P('slab', None, 'span')
All inputs are finite; a program needn't handle non-finite values.
Results may differ from a plain program's by a relative error of at most 0.00005.
Values sent between devices are 32-bit elements; how exact they have to be, the bound alone decides.
No kernel may reach another device: no remote copies, remote signals or barrier semaphores. Data moves between devices by JAX's collectives and lax.ppermute only.
A program may use at most 128 MiB of HBM per device.

v0:
```python
import math
import jax
import jax.numpy as jnp
from jax import lax
from jax.sharding import PartitionSpec as P


def tables(number, length, span_total):
    wavenumber = lax.iota(jnp.int32, number)
    position = lax.iota(jnp.int32, length)
    phases = wavenumber[:, None] * position[None, :] % span_total
    angles = phases.astype(jnp.float32) * (2.0 * math.pi / span_total)
    return (jnp.cos(angles), jnp.sin(angles))


def weighting(number, span_total):
    wavenumber = lax.iota(jnp.int32, number)
    return (jnp.where(wavenumber == 0, 1.0, 2.0) / span_total).astype(jnp.float32)[:, None]


def forward_modes(cos_table, sin_table, field_rows):
    highest = lax.Precision.HIGHEST
    part_real = jnp.einsum("mz,pz->mp", cos_table, field_rows, precision=highest)
    part_imag = -jnp.einsum("mz,pz->mp", sin_table, field_rows, precision=highest)
    return jnp.concatenate([part_real, part_imag], axis=1)


def inverse_modes(cos_table, sin_table, mode_data, scaling, row_width):
    highest = lax.Precision.HIGHEST
    first = jnp.einsum(
        "mp,mz->pz", mode_data[:, :row_width] * scaling, cos_table, precision=highest
    )
    second = jnp.einsum(
        "mp,mz->pz", mode_data[:, row_width:] * scaling, sin_table, precision=highest
    )
    return first - second


def mix_modes(spectrum, weights, row_count, channels):
    highest = lax.Precision.HIGHEST
    mode_count = spectrum.shape[0]
    parts = spectrum.reshape(mode_count, 2, row_count, channels)
    blocks = weights.reshape(mode_count, 2, channels, channels)
    spec_real = parts[:, 0]
    spec_imag = parts[:, 1]
    mixed_real = jnp.einsum(
        "mrc,mco->mro", spec_real, blocks[:, 0], precision=highest
    ) - jnp.einsum("mrc,mco->mro", spec_imag, blocks[:, 1], precision=highest)
    mixed_imag = jnp.einsum(
        "mrc,mco->mro", spec_real, blocks[:, 1], precision=highest
    ) + jnp.einsum("mrc,mco->mro", spec_imag, blocks[:, 0], precision=highest)
    return jnp.concatenate(
        [
            mixed_real.reshape(mode_count, row_count * channels),
            mixed_imag.reshape(mode_count, row_count * channels),
        ],
        axis=1,
    )


def shards(features, spectral_weight, local_weight, bias_vector):
    rows_dev, channels, span_cells = features.shape
    span_count = lax.axis_size("span")
    span_total = span_cells * span_count
    modes_dev = spectral_weight.shape[0]
    modes_all = modes_dev * span_count
    weights = lax.all_gather(spectral_weight, "slab", axis=1, tiled=True)
    whole_weights = lax.all_gather(weights, "span", axis=0, tiled=True)
    line_data = lax.all_to_all(features, "span", split_axis=0, concat_axis=2, tiled=True)
    line_count = line_data.shape[0]
    line_width = line_count * channels
    line_rows = line_data.reshape(line_width, span_total)
    cos_table, sin_table = tables(modes_all, span_total, span_total)
    spectrum = forward_modes(cos_table, sin_table, line_rows)
    mixed = mix_modes(spectrum, whole_weights, line_count, channels)
    scaling = weighting(modes_all, span_total)
    returned = inverse_modes(cos_table, sin_table, mixed, scaling, line_width)
    returned = returned.reshape(line_count, channels, span_total)
    spectral = lax.all_to_all(returned, "span", split_axis=2, concat_axis=0, tiled=True)
    local_term = jnp.einsum("rcz,co->roz", features, local_weight, precision=lax.Precision.HIGHEST)
    return jax.nn.gelu(spectral + local_term + bias_vector[None, :, None], approximate=False)


def solution(mesh):
    placed = (P("slab", None, "span"), P("span", "slab"), P(), P())
    return jax.shard_map(
        shards, mesh=mesh, in_specs=placed, out_specs=P("slab", None, "span"), check_vma=False
    )
```

profile of v0, /device:TPU:0, one launch (start us, length us, event | category | flops | bytes accessed | tf_op | source)
XLA Modules:
  0.0 531.0 jit_solution(9405047965576421890)
XLA Ops:
  6.5 0.0 copy-start
  6.5 0.0 copy-start.2
  6.5 7.4 %all-to-all-start = ((f32[128,32,256]{2,1,0:T(8,128)}), f32[128,32,256]{2,1,0:T(8,128)}, u32[]{:S(2)}, u32[]{:S(2)}) async-start(f32[128,32,256]{2,1,0:T(8,128)} %param.4), calls=%async_computation | async-start | bytes 8388608 | tf_op jit(solution)/shard_map/all_to_all | solution.py:69
  14.0 0.0 all-gather.2.cloned.1.call-start
  14.0 0.0 copy-done.2
  14.0 7.6 %all_gather.6 = f32[64,2048]{1,0:T(8,128)} all-gather(f32[64,512]{1,0:T(8,128)S(1)} %copy-done.2), channel_id=1, replica_groups=mesh['span'=8,'slab'=4] {'slab'}, dimensions={1}, use_global_device_ids=true | all-gather | bytes 655360 | tf_op jit(solution)/shard_map/all_gather | solution.py:67
  21.7 0.0 all-gather.2.cloned.1.call-update
  21.7 136.3 %all-to-all-done = f32[128,32,256]{2,1,0:T(8,128)} async-done(((f32[128,32,256]{2,1,0:T(8,128)}), f32[128,32,256]{2,1,0:T(8,128)}, u32[]{:S(2)}, u32[]{:S(2)}) %all-to-all-start) | async-done | bytes 4194336 | tf_op jit(solution)/shard_map/all_to_all | solution.py:69
  158.0 5.5 %copy.19 = f32[8,16,32,256]{3,0,2,1:T(8,128)S(1)} copy(f32[8,16,32,256]{3,2,1,0:T(8,128)} %bitcast) | data formatting | bytes 8388608 | tf_op jit(solution)/shard_map/all_to_all | solution.py:69
  163.5 2.0 copy.36
  165.5 22.5 %fusion.42 = f32[512,512]{0,1:T(8,128)S(1)} fusion(f32[512,2048]{1,0:T(8,128)S(1)} %bitcast.71), kind=kOutput, calls=%fused_computation.48 | convolution fusion | flops 6457131008 | bytes 5242880 | tf_op jit(solution)/shard_map/mz,pz->mp/dot_general | solution.py:23
  188.0 23.2 %fusion.47 = f32[512,512]{0,1:T(8,128)} fusion(f32[512,2048]{1,0:T(8,128)S(1)} %bitcast.72), kind=kOutput, calls=%fused_computation.50 | convolution fusion | flops 6457393152 | bytes 5242880 | tf_op jit(solution)/shard_map/mz,pz->mp/dot_general | solution.py:24
  211.1 0.0 all-gather.2.cloned.1.call-done
  211.1 5.5 %copy.21 = f32[512,2048]{0,1:T(8,128)} copy(f32[512,2048]{1,0:T(8,128)} %all-gather.2.cloned.1.call-done) | data formatting | bytes 8388608 | tf_op jit(solution)/shard_map/all_gather | solution.py:68
  216.6 4.2 fusion.67
  220.8 8.4 %copy.35 = f32[512,1,32,32]{3,2,0,1:T(8,128)} copy(f32[512,1,32,32]{0,3,2,1:T(8,128)} %get-tuple-element.6) | data formatting | bytes 4194304
  229.2 1.4 pad_maximum_fusion
  230.6 1.2 fusion.68
  231.9 4.6 copy.32
  236.5 7.6 %copy.33 = f32[512,1,32,32]{3,2,0,1:T(8,128)} copy(f32[512,1,32,32]{0,3,2,1:T(8,128)S(1)} %get-tuple-element.5) | data formatting | bytes 4194304
  244.1 3.7 copy.34
  247.7 0.0 copy-start.1
  247.7 0.0 slice-start
  247.7 10.2 %fusion = f32[512,16,32]{2,1,0:T(8,128)S(1)} fusion(f32[512,1,32,32]{3,2,0,1:T(8,128)} %copy.35, f32[512,1,16,32]{3,2,0,1:T(8,128)} %copy.32), kind=kOutput, calls=%fused_computation | convolution fusion | flops 100663296 | bytes 4194304 | tf_op jit(solution)/shard_map/mrc,mco->mro/dot_general | solution.py:49
  257.9 0.0 copy-done.1
  258.0 0.0 slice-start.1
  258.0 10.8 %fusion.2 = f32[512,16,32]{2,1,0:T(8,128)} fusion(f32[512,1,32,32]{3,2,0,1:T(8,128)} %copy.35, f32[512,1,16,32]{3,2,0,1:T(8,128)S(1)} %copy-done.1), kind=kOutput, calls=%fused_computation.2 | convolution fusion | flops 100663296 | bytes 4194304 | tf_op jit(solution)/shard_map/mrc,mco->mro/dot_general | solution.py:48
  268.8 0.0 slice-done
  268.8 0.0 slice-done.1
  268.8 9.3 %fusion.33 = f32[512,16,32]{2,1,0:T(8,128)} fusion(f32[512,16,32]{2,1,0:T(8,128)S(1)} %fusion, f32[512,1,32,32]{3,2,0,1:T(8,128)S(1)} %bitcast.64, f32[512,1,16,32]{3,2,0,1:T(8,128)S(1)} %copy-done.1), kind=kOutput, calls=%fused_computation.43 | convolution fusion | flops 100925440 | bytes 5242880 | tf_op jit(solution)/shard_map/mrc,mco->mro/dot_general | solution.py:51
  278.1 2.8 copy.26
  280.9 12.4 %fusion.28 = f32[512,16,32]{2,1,0:T(8,128)} fusion(f32[512,16,32]{2,1,0:T(8,128)} %fusion.2, f32[512,1,32,32]{3,2,0,1:T(8,128)} %copy.33, f32[512,1,16,32]{3,2,0,1:T(8,128)} %copy.32), kind=kOutput, calls=%fused_computation.42 | convolution fusion | flops 100925440 | bytes 5242880 | tf_op jit(solution)/shard_map/mrc,mco->mro/dot_general | solution.py:46
  293.3 2.8 copy.25
  296.1 0.3 bitcast_multiply_fusion
  296.4 23.5 %fusion.40 = f32[512,2048]{1,0:T(8,128)S(1)} fusion(f32[512,512]{0,1:T(8,128)S(1)} %get-tuple-element.10), kind=kOutput, calls=%fused_computation.47 | convolution fusion | flops 6457131008 | bytes 5242880 | tf_op jit(solution)/shard_map/mp,mz->pz/dot_general | solution.py:30
  319.9 24.2 %convolution_subtract_fusion = f32[512,2048]{1,0:T(8,128)} fusion(f32[512,2048]{1,0:T(8,128)S(1)} %fusion.40, f32[512,512]{0,1:T(8,128)S(1)} %get-tuple-element.9), kind=kOutput, calls=%fused_computation.41 | convolution fusion | flops 6458179584 | bytes 9437184 | tf_op jit(solution)/shard_map/mp,mz->pz/dot_general | solution.py:33
  344.1 12.5 %copy.27 = f32[16,32,2048]{1,0,2:T(8,128)} copy(f32[16,32,2048]{2,1,0:T(8,128)} %bitcast.70) | data formatting | bytes 8388608 | tf_op jit(solution)/shard_map/reshape | solution.py:78
  356.6 12.8 %reshape.33 = f32[8,1,131072]{2,1,0:T(1,128)} reshape(f32[2048,16,32]{2,1,0:T(8,128)} %bitcast.65) | data formatting | bytes 8388608
  369.4 97.7 %all_to_all.33 = f32[8,1,131072]{2,1,0:T(1,128)} all-to-all(f32[8,1,131072]{2,1,0:T(1,128)} %reshape.33), channel_id=1, replica_groups=mesh['span'=8,'slab'=4] {'span'}, dimensions={0} | all-to-all | bytes 8388608 | tf_op jit(solution)/shard_map/all_to_all | solution.py:79
  467.2 0.6 broadcast.41
  467.7 13.8 %reduce = f32[8,131072]{1,0:T(8,128)} reduce(f32[8,1,131072]{2,1,0:T(1,128)} %all_to_all.33, f32[]{:T(128)} %broadcast.41), dimensions={1}, to_apply=%all_to_all.27.reduce_sub_computation | reduce | bytes 8388612 | tf_op jit(solution)/shard_map/all_to_all | solution.py:79
  481.5 13.4 %reshape.34 = f32[2048,16,32]{2,1,0:T(8,128)} reshape(f32[8,131072]{1,0:T(8,128)} %reduce) | data formatting | bytes 8388608
  494.9 0.0 copy-start.3
  494.9 13.1 %copy.28 = f32[16,32,8,256]{3,1,0,2:T(8,128)} copy(f32[16,32,8,256]{1,0,3,2:T(8,128)} %bitcast.66) | data formatting | bytes 8388608 | tf_op jit(solution)/shard_map/all_to_all | solution.py:79
  507.9 0.0 copy-done
  507.9 0.0 copy-done.3
  507.9 16.0 %fusion.12 = f32[128,32,256]{2,1,0:T(8,128)} fusion(f32[16,32,8,256]{3,1,0,2:T(8,128)} %copy.28, f32[128,32,256]{2,1,0:T(8,128)} %param.4, f32[32]{0:T(128)S(1)} %copy-done.3, f32[32,32]{1,0:T(8,128)S(1)} %copy-done), kind=kOutput, calls=%fused_computation.16 | convolution fusion | flops 471859200 | bytes 12587136 | tf_op jit(solution)/shard_map/rcz,co->roz/dot_general | solution.py:80
  (2 shorter events, 0.0 us)
Async XLA Ops:
  6.5 501.4 %copy-start = (f32[32,32]{1,0:T(8,128)S(1)}, f32[32,32]{1,0:T(8,128)}, u32[]{:S(2)}) copy-start(f32[32,32]{1,0:T(8,128)} %param.6) | copy-start | bytes 12292
  6.5 7.5 %copy-start.2 = (f32[64,512]{1,0:T(8,128)S(1)}, f32[64,512]{1,0:T(8,128)}, u32[]{:S(2)}) copy-start(f32[64,512]{1,0:T(8,128)} %param.5) | copy-start | bytes 393220
  6.5 151.4 %all-to-all-start = ((f32[128,32,256]{2,1,0:T(8,128)}), f32[128,32,256]{2,1,0:T(8,128)}, u32[]{:S(2)}, u32[]{:S(2)}) async-start(f32[128,32,256]{2,1,0:T(8,128)} %param.4), calls=%async_computation | async-start | bytes 8388608 | tf_op jit(solution)/shard_map/all_to_all | solution.py:69
  14.0 197.2 %all-gather.2.cloned.1.call-start = ((), (), s32[]{:S(2)}) async-start(), calls=%async_computation.2 | async-start | bytes 4718592 | tf_op jit(solution)/shard_map/all_gather | solution.py:68
  247.7 10.2 %copy-start.1 = (f32[512,1,16,32]{3,2,0,1:T(8,128)S(1)}, f32[512,1,16,32]{3,2,0,1:T(8,128)}, u32[]{:S(2)}) copy-start(f32[512,1,16,32]{3,2,0,1:T(8,128)} %copy.34) | copy-start | bytes 3145732
  247.7 21.1 %slice-start = ((s8[8388608]{0:T(1024)(128)(4,1)}), s8[4194304]{0:T(1024)(128)(4,1)S(1)}, s32[]{:S(2)}) async-start(s8[8388608]{0:T(1024)(128)(4,1)} %bitcast.63), calls=%async_computation.3 | async-start | bytes 8388608
  258.0 10.9 %slice-start.1 = ((s8[8388608]{0:T(1024)(128)(4,1)}), s8[4194304]{0:T(1024)(128)(4,1)S(1)}, s32[]{:S(2)}) async-start(s8[8388608]{0:T(1024)(128)(4,1)} %bitcast.63), calls=%async_computation.4 | async-start | bytes 8388608
  494.9 13.1 %copy-start.3 = (f32[32]{0:T(128)S(1)}, f32[32]{0:T(128)}, u32[]{:S(2)}) copy-start(f32[32]{0:T(128)} %param.7) | copy-start | bytes 388
Sparse Core Ops, SparseCore 0:
  21.8 131.8 all-gather.1
where the time goes:
time: 537 us; the launch traced here: 531 us
  matrix products  152 us (28%)
  waiting for transfers between devices  136 us (25%)
  blocking collectives  105 us (20%)
  local copies, waits for them, and re-layouts  101 us (19%)
  other arithmetic  15.4 us (3%)
  between operations  13.7 us (3%)
  starting transfers between devices  7.45 us (1%)
    all_to_all x1, waiting for transfers between devices, shards(): lax.all_to_all(features, 'span', split_axis=0, concat_axis=2, tiled=True)  136 us
    all_to_all x1, blocking collectives, shards(): lax.all_to_all(returned, 'span', split_axis=2, concat_axis=0, tiled=True)  97.7 us
    unnamed x19, local copies, waits for them, and re-layouts  52.4 us
    dot_general x1, matrix products, inverse_modes(): jnp.einsum('mp,mz->pz', mode_data[:, row_width:] * scaling, sin_table, pr...  24.2 us
    dot_general x1, matrix products, inverse_modes(): jnp.einsum('mp,mz->pz', mode_data[:, :row_width] * scaling, cos_table, pr...  23.5 us
    dot_general x1, matrix products, forward_modes(): jnp.einsum('mz,pz->mp', sin_table, field_rows, precision=highest)  23.2 us
    dot_general x1, matrix products, forward_modes(): jnp.einsum('mz,pz->mp', cos_table, field_rows, precision=highest)  22.5 us
    dot_general x1, matrix products, shards(): jnp.einsum('rcz,co->roz', features, local_weight, precision=lax.Precision...  16 us
  transfers between devices with their start and end apart: 2, of which 1 were waited for; matrix products, arithmetic and copies ran while one was open for 10% of the time, Pallas kernels for 0%

commit v1 on v0

--- a/solution.py
+++ b/solution.py
@@ -3,6 +3,18 @@
 import jax.numpy as jnp
 from jax import lax
 from jax.sharding import PartitionSpec as P
+
+
+def row_carry(z, row_dim, x_part):
+    v1, t1 = (z.shape[:row_dim], z.shape[row_dim + 1 :])
+    m_next = z.reshape(*v1, x_part, -1, *t1)
+    return jnp.moveaxis(m_next, row_dim, 0)
+
+
+def use_sides(xx, where_dim):
+    aux = list(xx.shape[1:])
+    aux[where_dim] *= xx.shape[0]
+    return jnp.moveaxis(xx, 0, where_dim).reshape(aux)
 
 
 def tables(number, length, span_total):
@@ -66,7 +78,20 @@
     modes_all = modes_dev * span_count
     weights = lax.all_gather(spectral_weight, "slab", axis=1, tiled=True)
     whole_weights = lax.all_gather(weights, "span", axis=0, tiled=True)
-    line_data = lax.all_to_all(features, "span", split_axis=0, concat_axis=2, tiled=True)
+    block_last = lax.axis_size("span")
+    high = lax.axis_index("span")
+    reached, u_next = (block_last, high)
+    w_next = row_carry(features, 0, reached)
+    pile = [w_next[u_next]]
+    for h in range(1, reached):
+        arr_out = w_next[(u_next + h) % reached]
+        answer = lax.ppermute(
+            arr_out, "span", [(idx, (idx + h) % reached) for idx in range(reached)]
+        )
+        pile.append(answer)
+    found_now = jnp.stack(pile, axis=0)
+    w_next = found_now[(u_next - jnp.arange(reached)) % reached]
+    line_data = use_sides(w_next, 2)
     line_count = line_data.shape[0]
     line_width = line_count * channels
     line_rows = line_data.reshape(line_width, span_total)

time: 537 us -> 549 us (1.022)
  waiting for transfers between devices: 136 us -> 61.2 us
  blocking collectives: 105 us -> 159 us
  starting transfers between devices: 7.45 us -> 30.5 us
  local copies, waits for them, and re-layouts: 101 us -> 113 us
    all_to_all x1 -> x0, waiting for transfers between devices: 136 us -> none  [shards(): lax.all_to_all(features, 'span', split_axis=0, concat_axis=2, tiled=True)]
    ppermute x0 -> x7, waiting for transfers between devices: none -> 61.2 us  [shards(): lax.ppermute(arr_out, 'span', [(idx, (idx + h) % reached) for idx in rang...]
    all_to_all x1, blocking collectives: 97.7 us -> 149 us  [shards(): lax.all_to_all(returned, 'span', split_axis=2, concat_axis=0, tiled=True)]
    ppermute x0 -> x7, starting transfers between devices: none -> 30.5 us  [shards(): lax.ppermute(arr_out, 'span', [(idx, (idx + h) % reached) for idx in rang...]
    all_to_all x1 -> x0, starting transfers between devices: 7.41 us -> none  [shards(): lax.all_to_all(features, 'span', split_axis=0, concat_axis=2, tiled=True)]
    all_to_all x1 -> x0, local copies, waits for them, and re-layouts: 5.49 us -> none  [shards(): lax.all_to_all(features, 'span', split_axis=0, concat_axis=2, tiled=True)]
    transpose x0 -> x1, local copies, waits for them, and re-layouts: none -> 5.49 us  [use_sides(): return jnp.moveaxis(xx, 0, where_dim).reshape(aux)]
    unnamed x19 -> x25, local copies, waits for them, and re-layouts: 52.4 us -> 56.7 us
  transfers between devices with their start and end apart: 2 -> 8, of which waited for: 1 -> 3; matrix products, arithmetic and copies ran while one was open for 10% -> 14% of each run, Pallas kernels for 0% -> 0%
where the time goes in v1:
time: 549 us; the launch traced here: 542 us
  blocking collectives  159 us (29%)
  matrix products  150 us (27%)
  local copies, waits for them, and re-layouts  113 us (21%)
  waiting for transfers between devices  61.2 us (11%)
  starting transfers between devices  30.5 us (6%)
  other arithmetic  14.2 us (3%)
  between operations  13.9 us (3%)
    all_to_all x1, blocking collectives, shards(): lax.all_to_all(returned, 'span', split_axis=2, concat_axis=0, tiled=True)  149 us
    ppermute x7, waiting for transfers between devices, shards(): lax.ppermute(arr_out, 'span', [(idx, (idx + h) % reached) for idx in rang...  61.2 us
    unnamed x25, local copies, waits for them, and re-layouts  56.7 us
    ppermute x7, starting transfers between devices, shards(): lax.ppermute(arr_out, 'span', [(idx, (idx + h) % reached) for idx in rang...  30.5 us
    dot_general x1, matrix products, inverse_modes(): jnp.einsum('mp,mz->pz', mode_data[:, row_width:] * scaling, sin_table, pr...  24.2 us
    dot_general x1, matrix products, inverse_modes(): jnp.einsum('mp,mz->pz', mode_data[:, :row_width] * scaling, cos_table, pr...  23.4 us
    dot_general x1, matrix products, forward_modes(): jnp.einsum('mz,pz->mp', cos_table, field_rows, precision=highest)  22.7 us
    dot_general x1, matrix products, forward_modes(): jnp.einsum('mz,pz->mp', sin_table, field_rows, precision=highest)  22.3 us
  transfers between devices with their start and end apart: 8, of which 3 were waited for; matrix products, arithmetic and copies ran while one was open for 14% of the time, Pallas kernels for 0%

profile of v1, /device:TPU:0, one launch (start us, length us, event | category | flops | bytes accessed | tf_op | source)
XLA Modules:
  0.0 541.9 jit_solution(16425208556676676037)
XLA Ops:
  6.5 0.0 copy-start
  6.5 0.0 all-gather.2.cloned.1.call-start
  6.5 10.4 %all_gather.6 = f32[64,2048]{1,0:T(8,128)} all-gather(f32[64,512]{1,0:T(8,128)} %param.5), channel_id=1, replica_groups=mesh['span'=8,'slab'=4] {'slab'}, dimensions={1}, use_global_device_ids=true | all-gather | bytes 655360 | tf_op jit(solution)/shard_map/all_gather | solution.py:79
  16.9 0.0 all-gather.2.cloned.1.call-update
  17.0 3.4 dynamic-slice_bitcast_fusion
  20.4 1.5 collective-permute-start
  21.9 1.6 collective-permute-start.1
  23.4 2.6 collective-permute-start.2
  26.0 1.2 collective-permute-start.3
  27.2 2.6 collective-permute-start.4
  29.9 14.8 %collective-permute-done = f32[16,32,256]{2,1,0:T(8,128)S(1)} collective-permute-done((f32[16,32,256]{2,1,0:T(8,128)S(1)}, f32[16,32,256]{2,1,0:T(8,128)S(1)}, u32[]{:S(2)}, u32[]{:S(2)}) %collective-permute-start) | collective-permute-done | bytes 524320 | tf_op jit(solution)/shard_map/ppermute | solution.py:88
  44.6 8.5 %collective-permute-start.5 = (f32[16,32,256]{2,1,0:T(8,128)S(1)}, f32[16,32,256]{2,1,0:T(8,128)S(1)}, u32[]{:S(2)}, u32[]{:S(2)}) collective-permute-start(f32[16,32,256]{2,1,0:T(8,128)S(1)} %get-tuple-element.8), channel_id=1, source_target_pairs={{0,24},{4,28},{8,0},{12,4},{16,8},{20,12},{24,16},{28,20},{1,25},{... | collective-permute-start | bytes 1572872 | tf_op jit(solution)/shard_map/ppermute | solution.py:88
  53.2 0.8 bitcast_dynamic-update-slice_fusion.6
  54.0 0.0 collective-permute-done.1
  54.0 12.5 %collective-permute-start.6 = (f32[16,32,256]{2,1,0:T(8,128)S(1)}, f32[16,32,256]{2,1,0:T(8,128)S(1)}, u32[]{:S(2)}, u32[]{:S(2)}) collective-permute-start(f32[16,32,256]{2,1,0:T(8,128)S(1)} %get-tuple-element.7), channel_id=1, source_target_pairs={{0,28},{4,0},{8,4},{12,8},{16,12},{20,16},{24,20},{28,24},{1,29},{... | collective-permute-start | bytes 1572872 | tf_op jit(solution)/shard_map/ppermute | solution.py:88
  66.5 0.8 bitcast_dynamic-update-slice_fusion.5
  67.3 31.9 %collective-permute-done.2 = f32[16,32,256]{2,1,0:T(8,128)S(1)} collective-permute-done((f32[16,32,256]{2,1,0:T(8,128)S(1)}, f32[16,32,256]{2,1,0:T(8,128)S(1)}, u32[]{:S(2)}, u32[]{:S(2)}) %collective-permute-start.2) | collective-permute-done | bytes 524320 | tf_op jit(solution)/shard_map/ppermute | solution.py:88
  99.3 0.8 bitcast_dynamic-update-slice_fusion.4
  100.1 0.0 collective-permute-done.3
  100.1 0.8 bitcast_dynamic-update-slice_fusion.3
  100.9 0.0 collective-permute-done.4
  100.9 0.8 bitcast_dynamic-update-slice_fusion.2
  101.8 0.0 collective-permute-done.5
  101.8 0.8 bitcast_dynamic-update-slice_fusion.1
  102.6 14.5 %collective-permute-done.6 = f32[16,32,256]{2,1,0:T(8,128)S(1)} collective-permute-done((f32[16,32,256]{2,1,0:T(8,128)S(1)}, f32[16,32,256]{2,1,0:T(8,128)S(1)}, u32[]{:S(2)}, u32[]{:S(2)}) %collective-permute-start.6) | collective-permute-done | bytes 524320 | tf_op jit(solution)/shard_map/ppermute | solution.py:88
  117.1 0.8 bitcast_dynamic-update-slice_fusion
  117.9 5.0 gather_fusion
  122.9 5.5 %copy.28 = f32[16,32,8,256]{3,2,1,0:T(8,128)S(1)} copy(f32[16,32,8,256]{3,1,0,2:T(8,128)} %bitcast.98) | data formatting | bytes 8388608 | tf_op jit(solution)/shard_map/transpose | solution.py:17
  128.4 2.0 copy.45
  130.4 22.7 %fusion.42 = f32[512,512]{0,1:T(8,128)S(1)} fusion(f32[512,2048]{1,0:T(8,128)S(1)} %bitcast.102), kind=kOutput, calls=%fused_computation.49 | convolution fusion | flops 6457131008 | bytes 5242880 | tf_op jit(solution)/shard_map/mz,pz->mp/dot_general | solution.py:35
  153.1 22.3 %fusion.47 = f32[512,512]{0,1:T(8,128)S(1)} fusion(f32[512,2048]{1,0:T(8,128)S(1)} %bitcast.103), kind=kOutput, calls=%fused_computation.51 | convolution fusion | flops 6457393152 | bytes 5242880 | tf_op jit(solution)/shard_map/mz,pz->mp/dot_general | solution.py:36
  175.4 0.2 pad_maximum_fusion
  175.6 0.2 fusion.70
  175.8 3.9 copy.41
  179.7 3.7 copy.43
  183.4 0.0 all-gather.2.cloned.1.call-done
  183.4 5.3 copy.30
  188.7 4.2 fusion.69
  193.0 8.3 %copy.44 = f32[512,1,32,32]{3,2,0,1:T(8,128)} copy(f32[512,1,32,32]{0,3,2,1:T(8,128)} %get-tuple-element.6) | data formatting | bytes 4194304
  201.3 7.6 %copy.42 = f32[512,1,32,32]{3,2,0,1:T(8,128)} copy(f32[512,1,32,32]{0,3,2,1:T(8,128)S(1)} %get-tuple-element.5) | data formatting | bytes 4194304
  208.9 10.5 %fusion = f32[512,16,32]{2,1,0:T(8,128)S(1)} fusion(f32[512,1,32,32]{3,2,0,1:T(8,128)} %copy.44, f32[512,1,16,32]{3,2,0,1:T(8,128)} %copy.41), kind=kOutput, calls=%fused_computation.1 | convolution fusion | flops 100663296 | bytes 4194304 | tf_op jit(solution)/shard_map/mrc,mco->mro/dot_general | solution.py:61
  219.4 0.0 copy-done.1
  219.5 0.0 copy-done.2
  219.5 0.0 slice-start.1
  219.5 9.1 %fusion.2 = f32[512,16,32]{2,1,0:T(8,128)} fusion(f32[512,1,32,32]{3,2,0,1:T(8,128)S(1)} %copy-done.1, f32[512,1,16,32]{3,2,0,1:T(8,128)S(1)} %copy-done.2), kind=kOutput, calls=%fused_computation.3 | convolution fusion | flops 100663296 | bytes 4194304 | tf_op jit(solution)/shard_map/mrc,mco->mro/dot_general | solution.py:60
  228.6 0.0 slice-done
  228.6 0.0 slice-done.1
  228.6 9.5 %fusion.33 = f32[512,16,32]{2,1,0:T(8,128)} fusion(f32[512,16,32]{2,1,0:T(8,128)S(1)} %fusion, f32[512,1,32,32]{3,2,0,1:T(8,128)S(1)} %bitcast.94, f32[512,1,16,32]{3,2,0,1:T(8,128)S(1)} %copy-done.2), kind=kOutput, calls=%fused_computation.44 | convolution fusion | flops 100925440 | bytes 5242880 | tf_op jit(solution)/shard_map/mrc,mco->mro/dot_general | solution.py:63
  238.1 2.8 copy.35
  240.9 12.4 %fusion.28 = f32[512,16,32]{2,1,0:T(8,128)} fusion(f32[512,16,32]{2,1,0:T(8,128)} %fusion.2, f32[512,1,32,32]{3,2,0,1:T(8,128)} %copy.42, f32[512,1,16,32]{3,2,0,1:T(8,128)} %copy.41), kind=kOutput, calls=%fused_computation.43 | convolution fusion | flops 100925440 | bytes 5242880 | tf_op jit(solution)/shard_map/mrc,mco->mro/dot_general | solution.py:58
  253.3 2.8 copy.34
  256.1 0.3 bitcast_multiply_fusion
  256.3 23.4 %fusion.40 = f32[512,2048]{1,0:T(8,128)S(1)} fusion(f32[512,512]{0,1:T(8,128)S(1)} %get-tuple-element.18), kind=kOutput, calls=%fused_computation.48 | convolution fusion | flops 6457131008 | bytes 5242880 | tf_op jit(solution)/shard_map/mp,mz->pz/dot_general | solution.py:42
  279.8 24.2 %convolution_subtract_fusion = f32[512,2048]{1,0:T(8,128)} fusion(f32[512,2048]{1,0:T(8,128)S(1)} %fusion.40, f32[512,512]{0,1:T(8,128)S(1)} %get-tuple-element.17), kind=kOutput, calls=%fused_computation.42 | convolution fusion | flops 6458179584 | bytes 9437184 | tf_op jit(solution)/shard_map/mp,mz->pz/dot_general | solution.py:45
  304.0 12.5 %copy.36 = f32[16,32,2048]{1,0,2:T(8,128)} copy(f32[16,32,2048]{2,1,0:T(8,128)} %bitcast.101) | data formatting | bytes 8388608 | tf_op jit(solution)/shard_map/reshape | solution.py:103
  316.5 12.8 %reshape.89 = f32[8,1,131072]{2,1,0:T(1,128)} reshape(f32[2048,16,32]{2,1,0:T(8,128)} %bitcast.95) | data formatting | bytes 8388608
  329.3 148.7 %all_to_all.18 = f32[8,1,131072]{2,1,0:T(1,128)} all-to-all(f32[8,1,131072]{2,1,0:T(1,128)} %reshape.89), channel_id=1, replica_groups=mesh['span'=8,'slab'=4] {'span'}, dimensions={0} | all-to-all | bytes 8388608 | tf_op jit(solution)/shard_map/all_to_all | solution.py:104
  478.0 0.5 broadcast.117
  478.5 13.7 %reduce = f32[8,131072]{1,0:T(8,128)} reduce(f32[8,1,131072]{2,1,0:T(1,128)} %all_to_all.18, f32[]{:T(128)} %broadcast.117), dimensions={1}, to_apply=%all_to_all.13.reduce_sub_computation | reduce | bytes 8388612 | tf_op jit(solution)/shard_map/all_to_all | solution.py:104
  492.3 13.4 %reshape.90 = f32[2048,16,32]{2,1,0:T(8,128)} reshape(f32[8,131072]{1,0:T(8,128)} %reduce) | data formatting | bytes 8388608
  505.6 13.1 %copy.37 = f32[16,32,8,256]{3,1,0,2:T(8,128)} copy(f32[16,32,8,256]{1,0,3,2:T(8,128)} %bitcast.96) | data formatting | bytes 8388608 | tf_op jit(solution)/shard_map/all_to_all | solution.py:104
  518.7 0.0 copy-done
  518.7 0.0 copy-done.3
  518.7 16.1 %fusion.12 = f32[128,32,256]{2,1,0:T(8,128)} fusion(f32[16,32,8,256]{3,1,0,2:T(8,128)} %copy.37, f32[128,32,256]{2,1,0:T(8,128)} %param.4, f32[32]{0:T(128)S(1)} %copy-done.3, f32[32,32]{1,0:T(8,128)S(1)} %copy-done), kind=kOutput, calls=%fused_computation.17 | convolution fusion | flops 471859200 | bytes 12587136 | tf_op jit(solution)/shard_map/rcz,co->roz/dot_general | solution.py:105
  (8 shorter events, 0.0 us)
Async XLA Ops:
  6.5 512.2 %copy-start = (f32[32,32]{1,0:T(8,128)S(1)}, f32[32,32]{1,0:T(8,128)}, u32[]{:S(2)}) copy-start(f32[32,32]{1,0:T(8,128)} %param.6) | copy-start | bytes 12292
  6.5 176.9 %all-gather.2.cloned.1.call-start = ((), (), s32[]{:S(2)}) async-start(), calls=%async_computation.1 | async-start | bytes 4718592 | tf_op jit(solution)/shard_map/all_gather | solution.py:80
  20.4 24.3 %collective-permute-start = (f32[16,32,256]{2,1,0:T(8,128)S(1)}, f32[16,32,256]{2,1,0:T(8,128)S(1)}, u32[]{:S(2)}, u32[]{:S(2)}) collective-permute-start(f32[16,32,256]{2,1,0:T(8,128)S(1)} %get-tuple-element.13), channel_id=1, source_target_pairs={{0,4},{4,8},{8,12},{12,16},{16,20},{20,24},{24,28},{28,0},{1,5},{5... | collective-permute-start | bytes 1572872 | tf_op jit(solution)/shard_map/ppermute | solution.py:88
  21.9 32.2 %collective-permute-start.1 = (f32[16,32,256]{2,1,0:T(8,128)S(1)}, f32[16,32,256]{2,1,0:T(8,128)S(1)}, u32[]{:S(2)}, u32[]{:S(2)}) collective-permute-start(f32[16,32,256]{2,1,0:T(8,128)S(1)} %get-tuple-element.12), channel_id=1, source_target_pairs={{0,8},{4,12},{8,16},{12,20},{16,24},{20,28},{24,0},{28,4},{1,9},{5... | collective-permute-start | bytes 1572872 | tf_op jit(solution)/shard_map/ppermute | solution.py:88
  23.4 75.8 %collective-permute-start.2 = (f32[16,32,256]{2,1,0:T(8,128)S(1)}, f32[16,32,256]{2,1,0:T(8,128)S(1)}, u32[]{:S(2)}, u32[]{:S(2)}) collective-permute-start(f32[16,32,256]{2,1,0:T(8,128)S(1)} %get-tuple-element.11), channel_id=1, source_target_pairs={{0,12},{4,16},{8,20},{12,24},{16,28},{20,0},{24,4},{28,8},{1,13},{... | collective-permute-start | bytes 1572872 | tf_op jit(solution)/shard_map/ppermute | solution.py:88
  26.0 74.1 %collective-permute-start.3 = (f32[16,32,256]{2,1,0:T(8,128)S(1)}, f32[16,32,256]{2,1,0:T(8,128)S(1)}, u32[]{:S(2)}, u32[]{:S(2)}) collective-permute-start(f32[16,32,256]{2,1,0:T(8,128)S(1)} %get-tuple-element.10), channel_id=1, source_target_pairs={{0,16},{4,20},{8,24},{12,28},{16,0},{20,4},{24,8},{28,12},{1,17},{... | collective-permute-start | bytes 1572872 | tf_op jit(solution)/shard_map/ppermute | solution.py:88
  27.2 73.7 %collective-permute-start.4 = (f32[16,32,256]{2,1,0:T(8,128)S(1)}, f32[16,32,256]{2,1,0:T(8,128)S(1)}, u32[]{:S(2)}, u32[]{:S(2)}) collective-permute-start(f32[16,32,256]{2,1,0:T(8,128)S(1)} %get-tuple-element.9), channel_id=1, source_target_pairs={{0,20},{4,24},{8,28},{12,0},{16,4},{20,8},{24,12},{28,16},{1,21},{... | collective-permute-start | bytes 1572872 | tf_op jit(solution)/shard_map/ppermute | solution.py:88
  44.6 57.1 %collective-permute-start.5 = (f32[16,32,256]{2,1,0:T(8,128)S(1)}, f32[16,32,256]{2,1,0:T(8,128)S(1)}, u32[]{:S(2)}, u32[]{:S(2)}) collective-permute-start(f32[16,32,256]{2,1,0:T(8,128)S(1)} %get-tuple-element.8), channel_id=1, source_target_pairs={{0,24},{4,28},{8,0},{12,4},{16,8},{20,12},{24,16},{28,20},{1,25},{... | collective-permute-start | bytes 1572872 | tf_op jit(solution)/shard_map/ppermute | solution.py:88
  54.0 63.1 %collective-permute-start.6 = (f32[16,32,256]{2,1,0:T(8,128)S(1)}, f32[16,32,256]{2,1,0:T(8,128)S(1)}, u32[]{:S(2)}, u32[]{:S(2)}) collective-permute-start(f32[16,32,256]{2,1,0:T(8,128)S(1)} %get-tuple-element.7), channel_id=1, source_target_pairs={{0,28},{4,0},{8,4},{12,8},{16,12},{20,16},{24,20},{28,24},{1,29},{... | collective-permute-start | bytes 1572872 | tf_op jit(solution)/shard_map/ppermute | solution.py:88
  208.9 10.5 %copy-start.1 = (f32[512,1,32,32]{3,2,0,1:T(8,128)S(1)}, f32[512,1,32,32]{3,2,0,1:T(8,128)}, u32[]{:S(2)}) copy-start(f32[512,1,32,32]{3,2,0,1:T(8,128)} %copy.44) | copy-start | bytes 6291460
  208.9 10.5 %copy-start.2 = (f32[512,1,16,32]{3,2,0,1:T(8,128)S(1)}, f32[512,1,16,32]{3,2,0,1:T(8,128)}, u32[]{:S(2)}) copy-start(f32[512,1,16,32]{3,2,0,1:T(8,128)} %copy.43) | copy-start | bytes 3145732
  208.9 19.7 %slice-start = ((s8[8388608]{0:T(1024)(128)(4,1)}), s8[4194304]{0:T(1024)(128)(4,1)S(1)}, s32[]{:S(2)}) async-start(s8[8388608]{0:T(1024)(128)(4,1)} %bitcast.93), calls=%async_computation.2 | async-start | bytes 8388608
  219.5 9.1 %slice-start.1 = ((s8[8388608]{0:T(1024)(128)(4,1)}), s8[4194304]{0:T(1024)(128)(4,1)S(1)}, s32[]{:S(2)}) async-start(s8[8388608]{0:T(1024)(128)(4,1)} %bitcast.93), calls=%async_computation.3 | async-start | bytes 8388608
  505.6 13.1 %copy-start.3 = (f32[32]{0:T(128)S(1)}, f32[32]{0:T(128)}, u32[]{:S(2)}) copy-start(f32[32]{0:T(128)} %param.7) | copy-start | bytes 388
Sparse Core Ops, SparseCore 0:
  17.0 136.8 all-gather.1
